TPU v7x, 256 devices: a whole 4x4x8 slice. The times are simulated.
256 devices in a mesh: slot: 8 (over y_lo, x), feat: 32 (over y_hi, z, core).
Axes of the slice: x: 4, y: 4 (y_hi: 2, y_lo: 2; y = y_hi * 2 + y_lo), z: 8, core: 2. Of those that a mesh axis runs over, the one named last changes fastest.
Arguments:
- acts_in: bfloat16 [3, 256, 2304], P(None, None, 'slot'), may hold values from -6 to 6
- acts_out: bfloat16 [3, 256, 2304], P(None, None, 'slot'), may hold values from -6 to 6
- enc_weight: bfloat16 [3, 2304, 16384], P(None, 'slot', 'feat'), may hold values from -0.125 to 0.125
- enc_bias: float32 [3, 16384], P(None, 'feat'), may hold values from -3 to 3
- dec_weight: bfloat16 [6, 16384, 2304], P(None, 'feat', 'slot'), may hold values from -0.046875 to 0.046875
- dec_bias: float32 [3, 2304], P(None, 'slot'), may hold values from -3 to 3
Outputs:
- enc_grad: float32 [3, 2304, 16384], P(None, 'slot', 'feat')
- enc_bias_grad: float32 [3, 16384], P(None, 'feat')
- dec_grad: float32 [6, 16384, 2304], P(None, 'feat', 'slot')
- mse: float32 [], replicated
All inputs are finite; a program needn't handle non-finite values.
Results may differ from a plain program's by a relative error of at most 0.0095.
Values may be sent and summed in bfloat16 or wider, within the bound.
No kernel may reach another device: no remote copies, remote signals or barrier semaphores. Data moves between devices by JAX's collectives and lax.ppermute only.
A program may use at most 64 MiB of HBM per device.

v0:
```python
import functools
import jax
import jax.numpy as jnp
from jax import lax
from jax.sharding import Mesh
from jax.sharding import PartitionSpec as P

D = 2304
SLOT = ("slot_0", "slot_1")
FEAT = ("feat_0", "feat_1", "feat_2")
SLOT_FEAT = ("slot_0", "slot_1", "feat_0", "feat_1", "feat_2")


def cut_along(x, dim, devices):
    before, after = (x.shape[:dim], x.shape[dim + 1 :])
    return jnp.moveaxis(x.reshape(*before, devices, -1, *after), dim, 0)


def sum_at_owner(x, axis, dim):
    tiles = cut_along(x, dim, lax.axis_size(axis))
    arrived = lax.all_to_all(tiles, axis, split_axis=0, concat_axis=0, tiled=True)
    return arrived.sum(axis=0)


def over_axes(x, axes):
    return functools.reduce(lax.psum, axes, x)


def sent_to_all(x, axis):
    devices = lax.axis_size(axis)
    return lax.all_to_all(jnp.broadcast_to(x[None], (devices, *x.shape)), axis, 0, 0, tiled=True)


def joined_along(tiles, dim):
    dims = list(tiles.shape[1:])
    dims[dim] *= tiles.shape[0]
    return jnp.moveaxis(tiles, 0, dim).reshape(dims)


def collect(x, axis, dim):
    tiles = sent_to_all(x, axis)
    return joined_along(tiles, dim)


def activate(preact):
    return (
        jnp.maximum(preact, 0.0).astype(jnp.bfloat16),
        jnp.where(preact > 0, 1.0, 0.0).astype(jnp.bfloat16),
    )


def local(acts_in, acts_out, enc_weight, enc_bias, dec_weight, dec_bias):
    layers = acts_in.shape[0]
    tokens = acts_in.shape[1]
    width_dev = acts_in.shape[2]
    feature_dev = enc_weight.shape[2]
    pair_list = [(a, b) for a in range(layers) for b in range(a, layers)]

    def encode_rows():
        pieces = [
            jnp.dot(acts_in[a], enc_weight[a], preferred_element_type=jnp.float32)
            for a in range(layers)
        ]
        return jnp.concatenate(pieces, axis=1)

    bias_row = enc_bias.reshape(1, layers * feature_dev)
    preact = lax.psum(encode_rows(), SLOT) + bias_row
    features, slopes = activate(preact)
    target = (
        jnp.transpose(acts_out, (1, 0, 2)).reshape(tokens, layers * width_dev).astype(jnp.float32)
    )
    dec_row = dec_bias.reshape(1, layers * width_dev)
    portion = tokens // lax.axis_size(FEAT)
    row_block = features
    pieces = []
    for decode_b in range(layers):
        summed = jnp.zeros((portion * lax.axis_size(FEAT), width_dev), jnp.float32)
        for decode_a in range(decode_b + 1):
            pair_num = pair_list.index((decode_a, decode_b))
            summed = summed + jnp.dot(
                row_block[:, decode_a * feature_dev : (decode_a + 1) * feature_dev],
                dec_weight[pair_num],
                preferred_element_type=jnp.float32,
            )
        pieces.append(summed)
    rebuilt = sum_at_owner(jnp.concatenate(pieces, axis=1), FEAT, 0)
    offset = lax.axis_index(FEAT) * portion
    error_full = rebuilt + dec_row - lax.dynamic_slice_in_dim(target, offset, portion, 0)
    squared = over_axes(jnp.sum(error_full * error_full), SLOT_FEAT)
    error_half = collect(error_full.astype(jnp.bfloat16), FEAT, 0)
    mse = squared / (layers * tokens * D)
    dec_grads = []
    for a, b in pair_list:
        dec_grads.append(
            lax.dot_general(
                features[:, a * feature_dev : (a + 1) * feature_dev],
                error_half[:, b * width_dev : (b + 1) * width_dev],
                (((0,), (0,)), ((), ())),
                preferred_element_type=jnp.float32,
            )
        )
    row_block = error_half
    partials = []
    for upstream_a in range(layers):
        summed = jnp.zeros((tokens, feature_dev), jnp.float32)
        for b in range(upstream_a, layers):
            pair_num = pair_list.index((upstream_a, b))
            summed = summed + lax.dot_general(
                row_block[:, b * width_dev : (b + 1) * width_dev],
                dec_weight[pair_num],
                (((1,), (1,)), ((), ())),
                preferred_element_type=jnp.float32,
            )
        partials.append(summed)
    upstream = lax.psum(jnp.concatenate(partials, axis=1), SLOT)
    delta = upstream * slopes.astype(jnp.float32)
    bias_grad = jnp.sum(delta, axis=0).reshape(layers, feature_dev)
    delta_half = delta.astype(jnp.bfloat16)
    enc_grads = []
    for a in range(layers):
        enc_grads.append(
            lax.dot_general(
                acts_in[a],
                delta_half[:, a * feature_dev : (a + 1) * feature_dev],
                (((0,), (0,)), ((), ())),
                preferred_element_type=jnp.float32,
            )
        )
    return (jnp.stack(enc_grads), bias_grad, jnp.stack(dec_grads), mse)


def solution(mesh):
    split = Mesh(
        mesh.devices.reshape(2, 4, 2, 8, 2), ("slot_0", "slot_1", "feat_0", "feat_1", "feat_2")
    )
    in_specs = (
        P(None, None, SLOT),
        P(None, None, SLOT),
        P(None, SLOT, FEAT),
        P(None, FEAT),
        P(None, FEAT, SLOT),
        P(None, SLOT),
    )
    out_specs = (P(None, SLOT, FEAT), P(None, FEAT), P(None, FEAT, SLOT), P())
    return jax.shard_map(local, mesh=split, in_specs=in_specs, out_specs=out_specs, check_vma=False)
```

profile of v0, /device:TPU:32, one launch (start us, length us, event | category | flops | bytes accessed | tf_op | source)
XLA Modules:
  0.0 258.0 jit_solution(12020248933589295281)
XLA Ops:
  7.2 1.4 fusion.26
  8.6 1.4 fusion.28
  9.9 1.4 fusion.30
  11.3 1.3 pad_maximum_fusion.1
  12.6 87.5 %all-reduce.3.cloned.1.call-done = f32[256,1536]{1,0:T(8,128)} async-done(((f32[256,1536]{1,0:T(8,128)}), f32[256,1536]{1,0:T(8,128)}) %all-reduce.3.cloned.1.call-update) | async-done | bytes 1572880 | tf_op jit(solution)/shard_map/psum | solution.py:67
  100.1 1.6 maximum_convert_fusion
  101.7 0.3 fusion.14
  101.9 0.3 fusion.20
  102.2 0.3 fusion.24
  102.5 0.3 convolution_add_fusion.4
  102.8 0.3 convolution_add_fusion.3
  103.0 0.3 convolution_add_fusion.5
  103.3 0.1 pad_maximum_fusion.3
  103.4 1.2 copy.15
  104.6 9.8 %all-to-all-start = ((f32[32,8,864]{2,1,0:T(8,128)}), f32[32,8,864]{2,1,0:T(8,128)S(1)}, u32[]{:S(2)}, u32[]{:S(2)}) async-start(f32[32,8,864]{2,1,0:T(8,128)} %bitcast.107), calls=%async_computation | async-start | bytes 1835008 | tf_op jit(solution)/shard_map/all_to_all | solution.py:21
  114.5 2.0 convert_element_type.33
  116.5 2.0 constant_dynamic-slice_fusion
  118.5 1.2 copy.17
  119.6 0.1 add.67
  119.7 22.4 %all-to-all-done = f32[32,8,864]{2,1,0:T(8,128)S(1)} async-done(((f32[32,8,864]{2,1,0:T(8,128)}), f32[32,8,864]{2,1,0:T(8,128)S(1)}, u32[]{:S(2)}, u32[]{:S(2)}) %all-to-all-start) | async-done | bytes 884768 | tf_op jit(solution)/shard_map/all_to_all | solution.py:21
  142.1 0.1 reduce_sum.27
  142.2 0.6 multiply_reduce_fusion
  142.8 21.1 %all_to_all.10 = bf16[32,8,864]{2,1,0:T(8,128)(2,1)S(1)} all-to-all(bf16[32,8,864]{2,1,0:T(8,128)(2,1)S(1)} %broadcast_in_dim.12), channel_id=1, replica_groups=mesh['slot_0'=2,'slot_1'=4,'feat_0'=2,'feat_1'=8,'feat_2'=2] {'feat_0','..., dimensions={0} | all-to-all | bytes 884736 | tf_op jit(solution)/shard_map/all_to_all | solution.py:31
  163.9 0.3 fusion.22
  164.2 0.3 fusion.16
  164.6 0.3 fusion.8
  164.9 0.3 convolution_add_fusion.2
  165.3 0.3 convolution_add_fusion.1
  165.6 0.3 convolution_add_fusion
  166.0 1.3 pad_maximum_fusion.2
  167.3 5.6 %psum.51 = f32[]{:T(128)} all-reduce(f32[]{:T(128)} %get-tuple-element.6), channel_id=1, replica_groups=mesh['slot_0'=2,'slot_1'=4,'feat_0'=2,'feat_1'=8,'feat_2'=2] {'slot_0'}, use_global_device_ids=true, to_apply=%region_5.6 | all-reduce | flops 1 | bytes 8 | tf_op jit(solution)/shard_map/psum | solution.py:26
  172.8 9.6 %psum.52 = f32[]{:T(128)} all-reduce(f32[]{:T(128)} %psum.51), channel_id=1, replica_groups=mesh['slot_0'=2,'slot_1'=4,'feat_0'=2,'feat_1'=8,'feat_2'=2] {'slot_1'}, use_global_device_ids=true, to_apply=%region_6.7 | all-reduce | flops 1 | bytes 8 | tf_op jit(solution)/shard_map/psum | solution.py:26
  182.5 7.1 %psum.53 = f32[]{:T(128)} all-reduce(f32[]{:T(128)} %psum.52), channel_id=1, replica_groups=mesh['slot_0'=2,'slot_1'=4,'feat_0'=2,'feat_1'=8,'feat_2'=2] {'feat_0'}, use_global_device_ids=true, to_apply=%region_7.8 | all-reduce | flops 1 | bytes 8 | tf_op jit(solution)/shard_map/psum | solution.py:26
  189.5 15.8 %psum.54 = f32[]{:T(128)} all-reduce(f32[]{:T(128)} %psum.53), channel_id=1, replica_groups=mesh['slot_0'=2,'slot_1'=4,'feat_0'=2,'feat_1'=8,'feat_2'=2] {'feat_1'}, use_global_device_ids=true, to_apply=%region_8.9 | all-reduce | flops 1 | bytes 8 | tf_op jit(solution)/shard_map/psum | solution.py:26
  205.3 3.1 %psum.55 = f32[]{:T(128)} all-reduce(f32[]{:T(128)} %psum.54), channel_id=1, replica_groups=mesh['slot_0'=2,'slot_1'=4,'feat_0'=2,'feat_1'=8,'feat_2'=2] {'feat_2'}, use_global_device_ids=true, to_apply=%region_9.10 | all-reduce | flops 1 | bytes 8 | tf_op jit(solution)/shard_map/psum | solution.py:26
  209.0 1.1 fusion.5
  210.1 1.2 fusion.4
  211.3 1.2 fusion.3
  212.6 1.2 fusion.2
  213.8 1.2 fusion.1
  215.0 1.2 fusion
  216.2 29.3 %all-reduce.5.cloned.1.call-done = f32[256,1536]{1,0:T(8,128)} async-done(((f32[256,1536]{1,0:T(8,128)}), f32[256,1536]{1,0:T(8,128)}) %all-reduce.5.cloned.1.call-update) | async-done | bytes 1572880 | tf_op jit(solution)/shard_map/psum | solution.py:115
  245.5 1.8 fusion.6
  247.3 0.2 convolution_bitcast_fusion
  247.5 0.2 convolution_bitcast_fusion.1
  247.8 0.2 convolution_bitcast_fusion.2
  248.0 0.6 reshape.27
  248.6 1.3 pad_maximum_fusion
  (16 shorter events, 0.2 us)
Async XLA Ops:
  7.2 92.9 %all-reduce.3.cloned.1.call-start = ((), (), s32[]{:S(2)}) async-start(), calls=%async_computation.2 | async-start | bytes 3145728 | tf_op jit(solution)/shard_map/psum | solution.py:67
  11.3 1.3 copy-start.3
  12.6 89.1 %copy-start = (bf16[6,512,288]{1,2,0:T(8,128)(2,1)S(1)}, bf16[6,512,288]{1,2,0:T(8,128)(2,1)}, u32[]{:S(2)}) copy-start(bf16[6,512,288]{1,2,0:T(8,128)(2,1)} %param.10) | copy-start | bytes 5308420
  104.6 37.5 %all-to-all-start = ((f32[32,8,864]{2,1,0:T(8,128)}), f32[32,8,864]{2,1,0:T(8,128)S(1)}, u32[]{:S(2)}, u32[]{:S(2)}) async-start(f32[32,8,864]{2,1,0:T(8,128)} %bitcast.107), calls=%async_computation | async-start | bytes 1835008 | tf_op jit(solution)/shard_map/all_to_all | solution.py:21
  114.4 5.2 %copy-start.4 = (f32[3,288]{1,0:T(4,128)S(1)}, f32[3,288]{1,0:T(4,128)}, u32[]{:S(2)}) copy-start(f32[3,288]{1,0:T(4,128)} %param.11) | copy-start | bytes 10372
  114.4 131.1 %all-reduce.5.cloned.1.call-start = ((), (), s32[]{:S(2)}) async-start(), calls=%async_computation.3 | async-start | bytes 3145728 | tf_op jit(solution)/shard_map/psum | solution.py:115
  212.6 33.0 %copy-start.1 = (f32[256,1536]{1,0:T(8,128)S(1)}, f32[256,1536]{1,0:T(8,128)}, u32[]{:S(2)}) copy-start(f32[256,1536]{1,0:T(8,128)} %all-reduce.3.cloned.1.call-done) | copy-start | bytes 4718596
  216.2 31.1 %copy-start.2 = (bf16[3,256,288]{1,2,0:T(8,128)(2,1)S(1)}, bf16[3,256,288]{1,2,0:T(8,128)(2,1)}, u32[]{:S(2)}) copy-start(bf16[3,256,288]{1,2,0:T(8,128)(2,1)} %param.6) | copy-start | bytes 1327108
Sparse Core Ops, SparseCore 0:
  12.7 87.3 all-reduce.2
  167.4 78.1 all-reduce.4
where the time goes:
time: 259 us; the launch traced here: 258 us
  waiting for transfers between devices  139 us (54%)
  blocking collectives  62.2 us (24%)
  between operations  16 us (6%)
  matrix products  15.5 us (6%)
  other arithmetic  9.89 us (4%)
  starting transfers between devices  9.88 us (4%)
  local copies, waits for them, and re-layouts  5.13 us (2%)
    psum x1, waiting for transfers between devices, local(): preact = lax.psum(encode_rows(), SLOT) + bias_row  87.5 us
    psum x5, blocking collectives, over_axes(): return functools.reduce(lax.psum, axes, x)  41.1 us
    psum x1, waiting for transfers between devices, local(): upstream = lax.psum(jnp.concatenate(partials, axis=1), SLOT)  29.3 us
    all_to_all x1, waiting for transfers between devices, sum_at_owner(): lax.all_to_all(tiles, axis, split_axis=0, concat_axis=0, tiled=True)  22.4 us
    all_to_all x1, blocking collectives, sent_to_all(): lax.all_to_all(jnp.broadcast_to(x[None], (devices, *x.shape)), axis, 0, 0...  21.1 us
    all_to_all x1, starting transfers between devices, sum_at_owner(): lax.all_to_all(tiles, axis, split_axis=0, concat_axis=0, tiled=True)  9.8 us
    dot_general x6, matrix products, local(): lax.dot_general(features[:, a * feature_dev:(a + 1) * feature_dev], error...  7.18 us
  transfers between devices with their start and end apart: 3, of which 3 were waited for; matrix products, arithmetic and copies ran while one was open for 5% of the time, Pallas kernels for 0%

commit v1 on v0

--- a/solution.py
+++ b/solution.py
@@ -112,7 +112,9 @@
                 preferred_element_type=jnp.float32,
             )
         partials.append(summed)
-    upstream = lax.psum(jnp.concatenate(partials, axis=1), SLOT)
+    buf = jnp.concatenate(partials, axis=1)
+    side_arr = lax.all_gather(buf, axis_name=SLOT)
+    upstream = jnp.sum(side_arr, 0)
     delta = upstream * slopes.astype(jnp.float32)
     bias_grad = jnp.sum(delta, axis=0).reshape(layers, feature_dev)
     delta_half = delta.astype(jnp.bfloat16)

time: 259 us -> 316 us (1.22)
  waiting for transfers between devices: 139 us -> 188 us
  other arithmetic: 9.89 us -> 17.4 us
    all_gather x0 -> x1, waiting for transfers between devices: none -> 78.1 us  [local(): side_arr = lax.all_gather(buf, axis_name=SLOT)]
    psum x1 -> x0, waiting for transfers between devices: 29.3 us -> none  [local(): upstream = lax.psum(jnp.concatenate(partials, axis=1), SLOT)]
    reduce_sum x0 -> x1, other arithmetic: none -> 7.41 us  [local(): upstream = jnp.sum(side_arr, 0)]
  transfers between devices with their start and end apart: 3 -> 3, of which waited for: 3 -> 3; matrix products, arithmetic and copies ran while one was open for 5% -> 4% of each run, Pallas kernels for 0% -> 0%
where the time goes in v1:
time: 316 us; the launch traced here: 315 us
  waiting for transfers between devices  188 us (59%)
  blocking collectives  62.7 us (20%)
  other arithmetic  17.4 us (6%)
  between operations  16.1 us (5%)
  matrix products  15.5 us (5%)
  starting transfers between devices  9.9 us (3%)
  local copies, waits for them, and re-layouts  5.1 us (2%)
    psum x1, waiting for transfers between devices, local(): preact = lax.psum(encode_rows(), SLOT) + bias_row  87.4 us
    all_gather x1, waiting for transfers between devices, local(): side_arr = lax.all_gather(buf, axis_name=SLOT)  78.1 us
    psum x5, blocking collectives, over_axes(): return functools.reduce(lax.psum, axes, x)  41.6 us
    all_to_all x1, waiting for transfers between devices, sum_at_owner(): lax.all_to_all(tiles, axis, split_axis=0, concat_axis=0, tiled=True)  22.4 us
    all_to_all x1, blocking collectives, sent_to_all(): lax.all_to_all(jnp.broadcast_to(x[None], (devices, *x.shape)), axis, 0, 0...  21.1 us
    all_to_all x1, starting transfers between devices, sum_at_owner(): lax.all_to_all(tiles, axis, split_axis=0, concat_axis=0, tiled=True)  9.82 us
    reduce_sum x1, other arithmetic, local(): upstream = jnp.sum(side_arr, 0)  7.41 us
    dot_general x6, matrix products, local(): lax.dot_general(features[:, a * feature_dev:(a + 1) * feature_dev], error...  7.18 us
  transfers between devices with their start and end apart: 3, of which 3 were waited for; matrix products, arithmetic and copies ran while one was open for 4% of the time, Pallas kernels for 0%

profile of v1, /device:TPU:32, one launch (start us, length us, event | category | flops | bytes accessed | tf_op | source)
XLA Modules:
  0.0 314.6 jit_solution(5127203212242815642)
XLA Ops:
  7.2 1.4 fusion.30
  8.6 1.4 fusion.26
  9.9 1.4 fusion.28
  11.3 1.3 pad_maximum_fusion.1
  12.6 87.4 %all-reduce.2.cloned.1.call-done = f32[256,1536]{1,0:T(8,128)} async-done(((f32[256,1536]{1,0:T(8,128)}), f32[256,1536]{1,0:T(8,128)}) %all-reduce.2.cloned.1.call-update) | async-done | bytes 1572880 | tf_op jit(solution)/shard_map/psum | solution.py:67
  100.1 1.6 maximum_convert_fusion
  101.6 0.3 fusion.20
  101.9 0.3 fusion.14
  102.2 0.3 fusion.24
  102.5 0.3 convolution_add_fusion.5
  102.7 0.3 convolution_add_fusion.4
  103.0 0.3 convolution_add_fusion.3
  103.4 1.2 copy.15
  104.6 9.8 %all-to-all-start = ((f32[32,8,864]{2,1,0:T(8,128)}), f32[32,8,864]{2,1,0:T(8,128)S(1)}, u32[]{:S(2)}, u32[]{:S(2)}) async-start(f32[32,8,864]{2,1,0:T(8,128)} %bitcast.109), calls=%async_computation | async-start | bytes 1835008 | tf_op jit(solution)/shard_map/all_to_all | solution.py:21
  114.5 0.1 add.65
  114.6 2.0 convert_element_type.33
  116.6 2.0 constant_dynamic-slice_fusion
  118.5 1.2 copy.17
  119.7 22.4 %all-to-all-done = f32[32,8,864]{2,1,0:T(8,128)S(1)} async-done(((f32[32,8,864]{2,1,0:T(8,128)}), f32[32,8,864]{2,1,0:T(8,128)S(1)}, u32[]{:S(2)}, u32[]{:S(2)}) %all-to-all-start) | async-done | bytes 884768 | tf_op jit(solution)/shard_map/all_to_all | solution.py:21
  142.1 0.1 reduce_sum.36
  142.2 0.6 multiply_reduce_fusion
  142.8 21.1 %all_to_all.10 = bf16[32,8,864]{2,1,0:T(8,128)(2,1)S(1)} all-to-all(bf16[32,8,864]{2,1,0:T(8,128)(2,1)S(1)} %broadcast_in_dim.12), channel_id=1, replica_groups=mesh['slot_0'=2,'slot_1'=4,'feat_0'=2,'feat_1'=8,'feat_2'=2] {'feat_0','..., dimensions={0} | all-to-all | bytes 884736 | tf_op jit(solution)/shard_map/all_to_all | solution.py:31
  163.9 0.3 fusion.8
  164.3 0.3 fusion.16
  164.6 0.3 fusion.22
  164.9 0.3 convolution_add_fusion
  165.3 0.3 convolution_add_fusion.2
  165.6 0.3 convolution_add_fusion.1
  166.0 1.3 pad_maximum_fusion.2
  167.2 5.6 %psum.43 = f32[]{:T(128)} all-reduce(f32[]{:T(128)} %get-tuple-element.6), channel_id=1, replica_groups=mesh['slot_0'=2,'slot_1'=4,'feat_0'=2,'feat_1'=8,'feat_2'=2] {'slot_0'}, use_global_device_ids=true, to_apply=%region_5.6 | all-reduce | flops 1 | bytes 8 | tf_op jit(solution)/shard_map/psum | solution.py:26
  172.8 9.7 %psum.44 = f32[]{:T(128)} all-reduce(f32[]{:T(128)} %psum.43), channel_id=1, replica_groups=mesh['slot_0'=2,'slot_1'=4,'feat_0'=2,'feat_1'=8,'feat_2'=2] {'slot_1'}, use_global_device_ids=true, to_apply=%region_6.7 | all-reduce | flops 1 | bytes 8 | tf_op jit(solution)/shard_map/psum | solution.py:26
  182.5 7.4 %psum.45 = f32[]{:T(128)} all-reduce(f32[]{:T(128)} %psum.44), channel_id=1, replica_groups=mesh['slot_0'=2,'slot_1'=4,'feat_0'=2,'feat_1'=8,'feat_2'=2] {'feat_0'}, use_global_device_ids=true, to_apply=%region_7.8 | all-reduce | flops 1 | bytes 8 | tf_op jit(solution)/shard_map/psum | solution.py:26
  189.9 15.8 %psum.46 = f32[]{:T(128)} all-reduce(f32[]{:T(128)} %psum.45), channel_id=1, replica_groups=mesh['slot_0'=2,'slot_1'=4,'feat_0'=2,'feat_1'=8,'feat_2'=2] {'feat_1'}, use_global_device_ids=true, to_apply=%region_8.9 | all-reduce | flops 1 | bytes 8 | tf_op jit(solution)/shard_map/psum | solution.py:26
  205.7 3.1 psum.47
  209.5 1.1 fusion.5
  210.6 1.2 fusion.4
  211.8 1.2 fusion.3
  213.0 1.2 fusion.2
  214.2 1.2 fusion.1
  215.4 1.2 fusion
  216.6 78.1 %all-gather.3.cloned.1.call-done = f32[2048,1536]{1,0:T(8,128)} async-done(((f32[256,1536]{1,0:T(8,128)}), f32[2048,1536]{1,0:T(8,128)}) %all-gather.3.cloned.1.call-update) | async-done | bytes 12582928 | tf_op jit(solution)/shard_map/all_gather | solution.py:116
  294.7 7.4 %reduce_sum.37 = f32[256,1536]{1,0:T(8,128)} reduce(f32[8,256,1536]{2,1,0:T(8,128)} %bitcast.108, f32[]{:T(128)} %constant.11.clone.1), dimensions={0}, to_apply=%region_2.3 | reduce | flops 2752512 | bytes 14155780 | tf_op jit(solution)/shard_map/reduce_sum | solution.py:117
  302.1 1.8 fusion.6
  303.9 0.2 convolution_bitcast_fusion
  304.2 0.2 convolution_bitcast_fusion.1
  304.4 0.2 convolution_bitcast_fusion.2
  304.6 0.6 reshape.27
  305.3 1.3 pad_maximum_fusion
  (17 shorter events, 0.2 us)
Async XLA Ops:
  7.2 92.9 %all-reduce.2.cloned.1.call-start = ((), (), s32[]{:S(2)}) async-start(), calls=%async_computation.2 | async-start | bytes 3145728 | tf_op jit(solution)/shard_map/psum | solution.py:67
  11.3 1.3 copy-start.3
  12.6 89.1 %copy-start = (bf16[6,512,288]{1,2,0:T(8,128)(2,1)S(1)}, bf16[6,512,288]{1,2,0:T(8,128)(2,1)}, u32[]{:S(2)}) copy-start(bf16[6,512,288]{1,2,0:T(8,128)(2,1)} %param.10) | copy-start | bytes 5308420
  103.3 11.1 %copy-start.4 = (f32[3,288]{1,0:T(4,128)S(1)}, f32[3,288]{1,0:T(4,128)}, u32[]{:S(2)}) copy-start(f32[3,288]{1,0:T(4,128)} %param.11) | copy-start | bytes 10372
  104.6 37.5 %all-to-all-start = ((f32[32,8,864]{2,1,0:T(8,128)}), f32[32,8,864]{2,1,0:T(8,128)S(1)}, u32[]{:S(2)}, u32[]{:S(2)}) async-start(f32[32,8,864]{2,1,0:T(8,128)} %bitcast.109), calls=%async_computation | async-start | bytes 1835008 | tf_op jit(solution)/shard_map/all_to_all | solution.py:21
  114.4 180.3 %all-gather.3.cloned.1.call-start = ((), (), s32[]{:S(2)}) async-start(), calls=%async_computation.3 | async-start | bytes 14155776 | tf_op jit(solution)/shard_map/all_gather | solution.py:116
  294.7 7.4 %copy-start.1 = (f32[256,1536]{1,0:T(8,128)S(1)}, f32[256,1536]{1,0:T(8,128)}, u32[]{:S(2)}) copy-start(f32[256,1536]{1,0:T(8,128)} %all-reduce.2.cloned.1.call-done) | copy-start | bytes 4718596
  302.1 1.8 copy-start.2
Sparse Core Ops, SparseCore 0:
  12.7 87.3 all-reduce.1
  167.4 127.2 all-gather.2
